TPU v7x, 128 devices: a whole 4x4x4 slice. The times are simulated.
128 devices in a mesh: row: 8 (over x, core), col: 16 (over y, z).
Axes of the slice: x: 4, y: 4, z: 4, core: 2. Of those that a mesh axis runs over, the one named last changes fastest.
Arguments:
- amp_ladder: bfloat16 [8, 32, 128, 32, 128], P('row', 'col'), may hold values from -6 to 6
- integrals: bfloat16 [8, 24, 128, 32, 128], P(None, 'row', None, 'col'), may hold values from -0.09375 to 0.09375
- residual_in: float32 [8, 24, 128, 32, 128], P(None, 'row', None, 'col'), may hold values from -6 to 6
Outputs:
- residual_out: float32 [8, 24, 128, 32, 128], P(None, 'row', None, 'col')
All inputs are finite; a program needn't handle non-finite values.
Results may differ from a plain program's by a relative error of at most 0.0003.
Values may be sent and summed in bfloat16 or wider, within the bound.
A program may use at most 192 MiB of HBM per device.

v0:
```python
import jax
import jax.numpy as jnp
from jax import lax
from jax.sharding import PartitionSpec as P


def per_device(amp_ladder, integrals, residual_in):
    irreps = integrals.shape[0]
    row_blocks = integrals.shape[1]
    block = integrals.shape[2]
    row_count = row_blocks * block
    moved = lax.all_to_all(amp_ladder, "col", split_axis=3, concat_axis=1, tiled=True)
    cycle_amps = lax.all_gather(moved, "row", axis=0, tiled=True)
    col_local = cycle_amps.shape[3]
    shard_piece = lax.all_gather(integrals, "col", axis=3, tiled=True)
    width_now = shard_piece.shape[3]
    left_part = shard_piece.reshape(irreps, row_count, width_now * block)
    right_part = cycle_amps
    right_part = right_part.reshape(irreps, width_now * block, col_local * block)
    summed = jnp.einsum("hik,hkj->hij", left_part, right_part, preferred_element_type=jnp.float32)
    cycle_term = summed.reshape(irreps, row_blocks, block, col_local, block)
    return residual_in + cycle_term


def solution(mesh):
    placed = (
        P("row", "col", None, None, None),
        P(None, "row", None, "col", None),
        P(None, "row", None, "col", None),
    )
    return jax.shard_map(
        per_device,
        mesh=mesh,
        in_specs=placed,
        out_specs=P(None, "row", None, "col", None),
        check_vma=False,
    )
```

profile of v0, /device:TPU:3, one launch (start us, length us, event | category | flops | bytes accessed | tf_op | source)
XLA Modules:
  0.0 384.2 jit_solution(3818005593218872681)
XLA Ops:
  6.5 0.0 all-gather.5.cloned.1.call-start
  6.5 2.4 copy.7
  8.9 34.1 %all_to_all.18 = bf16[1,2,128,32,128]{4,2,1,0,3:T(8,128)(2,1)S(1)} all-to-all(bf16[1,2,128,32,128]{4,2,1,0,3:T(8,128)(2,1)S(1)} %copy.7), channel_id=1, replica_groups=mesh['row'=8,'col'=16] {'col'}, dimensions={3} | all-to-all | bytes 4194304 | tf_op jit(solution)/shard_map/all_to_all | solution.py:12
  43.0 1.5 copy.8
  44.5 0.0 all-gather.5.cloned.1.call-update
  44.5 0.0 all-gather.3.cloned.1.call-start
  44.5 2.9 copy.5
  47.5 0.0 all-gather.3.cloned.1.call-update
  47.5 82.3 %all-gather.5.cloned.1.call-done = bf16[8,32,128,2,128]{4,2,3,1,0:T(8,128)(2,1)} async-done(((bf16[1,32,128,2,128]{4,2,3,1,0:T(8,128)(2,1)}), bf16[8,32,128,2,128]{4,2,3,1,0:T(8,128)(2,1)}) %all-gather.5.cloned.1.call-update) | async-done | bytes 16777232 | tf_op jit(solution)/shard_map/all_gather | solution.py:13
  129.8 30.8 %copy.9 = bf16[8,32,128,2,128]{4,3,2,1,0:T(2,128)(2,1)} copy(bf16[8,32,128,2,128]{4,2,3,1,0:T(8,128)(2,1)} %all-gather.5.cloned.1.call-done) | data formatting | bytes 33554432 | tf_op jit(solution)/shard_map/all_gather | solution.py:13
  160.6 27.4 %reshape.10 = bf16[8,4096,256]{2,1,0:T(8,128)(2,1)} reshape(bf16[8,32,128,2,128]{4,3,2,1,0:T(2,128)(2,1)} %copy.9) | data formatting | bytes 33554432 | tf_op jit(solution)/shard_map/reshape | solution.py:19
  188.0 98.9 %all-gather.3.cloned.1.call-done = bf16[8,3,128,32,128]{4,2,1,0,3:T(8,128)(2,1)} async-done(((bf16[8,3,128,2,128]{4,2,1,0,3:T(8,128)(2,1)}), bf16[8,3,128,32,128]{4,2,1,0,3:T(8,128)(2,1)}) %all-gather.3.cloned.1.call-update) | async-done | bytes 25165840 | tf_op jit(solution)/shard_map/all_gather | solution.py:15
  286.9 26.8 %copy.6 = bf16[8,3,128,32,128]{4,3,2,1,0:T(8,128)(2,1)} copy(bf16[8,3,128,32,128]{4,2,1,0,3:T(8,128)(2,1)} %all-gather.3.cloned.1.call-done) | data formatting | bytes 50331648 | tf_op jit(solution)/shard_map/all_gather | solution.py:15
  313.7 37.4 %reshape.9 = bf16[8,384,4096]{2,1,0:T(8,128)(2,1)} reshape(bf16[8,3,128,32,128]{4,3,2,1,0:T(8,128)(2,1)} %copy.6) | data formatting | bytes 50331648 | tf_op jit(solution)/shard_map/reshape | solution.py:17
  351.1 17.5 %fusion = f32[8,384,256]{2,1,0:T(8,128)} fusion(bf16[8,384,4096]{2,1,0:T(8,128)(2,1)} %reshape.9, bf16[8,4096,256]{2,1,0:T(8,128)(2,1)} %reshape.10), kind=kOutput, calls=%fused_computation | convolution fusion | flops 6442450944 | bytes 45088768 | tf_op jit(solution)/shard_map/hik,hkj->hij/dot_general | solution.py:20
  368.6 3.5 reshape.11
  372.1 5.2 %add.3 = f32[8,3,128,2,128]{4,3,2,1,0:T(2,128)} add(f32[8,3,128,2,128]{4,3,2,1,0:T(2,128)} %param.5, f32[8,3,128,2,128]{4,3,2,1,0:T(2,128)S(1)} %reshape.11) | non-fusion elementwise | flops 786432 | bytes 9437184 | tf_op jit(solution)/shard_map/add | solution.py:22
Async XLA Ops:
  6.5 123.3 %all-gather.5.cloned.1.call-start = ((), (), s32[]{:S(2)}) async-start(), calls=%async_computation.2 | async-start | bytes 18874368 | tf_op jit(solution)/shard_map/all_gather | solution.py:13
  44.5 242.4 %all-gather.3.cloned.1.call-start = ((), (), s32[]{:S(2)}) async-start(), calls=%async_computation.1 | async-start | bytes 26738688 | tf_op jit(solution)/shard_map/all_gather | solution.py:15
Sparse Core Ops, SparseCore 0:
  44.6 85.1 all-gather.4
  132.0 154.8 all-gather.2
where the time goes:
time: 387 us; the launch traced here: 384 us
  waiting for transfers between devices  181 us (47%)
  local copies, waits for them, and re-layouts  133 us (34%)
  blocking collectives  34.1 us (9%)
  matrix products  17.5 us (5%)
  between operations  13.4 us (3%)
  other arithmetic  5.18 us (1%)
    all_gather x1, waiting for transfers between devices, per_device(): shard_piece = lax.all_gather(integrals, 'col', axis=3, tiled=True)  98.9 us
    all_gather x1, waiting for transfers between devices, per_device(): cycle_amps = lax.all_gather(moved, 'row', axis=0, tiled=True)  82.3 us
    reshape x1, local copies, waits for them, and re-layouts, per_device(): left_part = shard_piece.reshape(irreps, row_count, width_now * block)  37.4 us
    all_to_all x1, blocking collectives, per_device(): lax.all_to_all(amp_ladder, 'col', split_axis=3, concat_axis=1, tiled=True)  34.1 us
    all_gather x1, local copies, waits for them, and re-layouts, per_device(): cycle_amps = lax.all_gather(moved, 'row', axis=0, tiled=True)  30.8 us
    reshape x1, local copies, waits for them, and re-layouts, per_device(): right_part.reshape(irreps, width_now * block, col_local * block)  27.4 us
    all_gather x1, local copies, waits for them, and re-layouts, per_device(): shard_piece = lax.all_gather(integrals, 'col', axis=3, tiled=True)  26.8 us
    dot_general x1, matrix products, per_device(): jnp.einsum('hik,hkj->hij', left_part, right_part, preferred_element_type=...  17.5 us
  transfers between devices with their start and end apart: 2, of which 2 were waited for; matrix products, arithmetic and copies ran while one was open for 16% of the time, Pallas kernels for 0%

commit v1 on v0

v1 whole, which is shorter than its diff:
```python
import functools

import jax
import jax.numpy as jnp
from jax import lax
from jax.experimental import pallas as pl
from jax.experimental.pallas import tpu as pltpu
from jax.sharding import PartitionSpec as P

MESH = pl.DeviceIdType.MESH
JXOR = (1, 2, 0, 3)


def kernel(a_in, b_in, res, out, abuf, bbuf, cp, cr, cf, obuf,
           a_s, a_r, g_s, g_r, b_s, b_r, f_s, p_s, p_r, o_s, o_r):
    row, col = lax.axis_index("row"), lax.axis_index("col")
    x, c, y, z = row // 2, row % 2, col // 4, col % 4
    par = z // 2
    mir = 3 - z
    buddy = z + 1 - 2 * (z % 2)

    def dev(xx, cc, yy, zz):
        return (xx * 2 + cc, yy * 4 + zz)

    def xor(zz, j):
        lo, hi = zz % 2, zz // 2
        m = JXOR[j]
        lo = 1 - lo if m % 2 else lo
        hi = 1 - hi if m // 2 else hi
        return hi * 2 + lo

    def remote(src, dst, ss, rs, d):
        return pltpu.make_async_remote_copy(src, dst, ss, rs, device_id=d, device_id_type=MESH)

    barrier = pltpu.get_barrier_semaphore()
    peers = []
    for d in range(4):
        for zz in (z, mir):
            if d or zz is mir:
                peers.append(dev((x + d) % 4, c, y, zz))
            if d:
                peers.append(dev(x, c, (y + d) % 4, zz))
    peers.append(dev(x, 1 - c, y, z))
    peers.append(dev(x, c, y, buddy))
    for d in peers:
        pl.semaphore_signal(barrier, inc=1, device_id=d, device_id_type=MESH)
    pl.semaphore_wait(barrier, len(peers))

    sends = []

    def b_start(j):
        for dy in (1, 3, 2, 0):
            yd = (y + dy) % 4

            def go(zd, zz, local):
                src = b_in.at[yd * 4 + xor(zd, j)]
                dst = bbuf.at[j, pl.ds(pl.multiple_of((y * 2 + zz) * 256, 256), 256)]
                if local:
                    pltpu.make_async_copy(src, dst, b_r.at[y, zz, j]).start()
                else:
                    remote(src, dst, b_s.at[dy, j], b_r.at[y, zz, j], dev(x, c, yd, zd)).start()

            @pl.when(c == par)
            def _():
                go(z, 0, dy == 0)

            @pl.when(c != par)
            def _():
                go(mir, 1, False)

    def b_wait_sends():
        for j in range(4):
            for dy in range(4):
                cp_ = remote(b_in.at[0], bbuf.at[0, pl.ds(0, 256)], b_s.at[dy, j], b_r.at[0, 0, j], dev(x, c, y, z))
                if dy == 0:
                    @pl.when(c != par)
                    def _():
                        cp_.wait_send()
                else:
                    cp_.wait_send()

    def b_arrive(j):
        for dy in (0, 1, 3, 2):
            ys = (y + dy) % 4
            for zz in range(2):
                blk = bbuf.at[j, pl.ds(pl.multiple_of((ys * 2 + zz) * 256, 256), 256)]
                fw = remote(blk, blk, f_s.at[dy, zz, j], b_r.at[ys, zz, j], dev(x, 1 - c, y, z))
                fw.wait_recv()

                @pl.when(c == par)
                def _():
                    fw.start()

    def b_forward_wait():
        @pl.when(c == par)
        def _():
            for j in range(4):
                for dy in range(4):
                    for zz in range(2):
                        blk = bbuf.at[j, pl.ds(0, 256)]
                        remote(blk, blk, f_s.at[dy, zz, j], b_r.at[0, zz, j], dev(x, 1 - c, y, z)).wait_send()

    def a_copy(dx, zz):
        hx = (x + 4 - dx) % 4
        zd = mir if zz else z
        src = a_in.at[hx * 2 + zd // 2]
        dst = abuf.at[x, y * 2 + zz]
        if dx == 0 and zz == 0:
            return pltpu.make_async_copy(src, dst, a_r.at[x, 0])
        return remote(src, dst, a_s.at[dx, zz], a_r.at[x, zz], dev(hx, c, y, zd))

    def a_start(dx):
        for zz in (1, 0):
            cp_ = a_copy(dx, zz)
            cp_.start()
            if dx or zz:
                sends.append(cp_)

    def a_arrive(s):
        xs = (x + s) % 4
        for zz in range(2):
            blk = abuf.at[xs, y * 2 + zz]
            if s == 0 and zz == 0:
                a_copy(0, 0).wait()
            else:
                remote(blk, blk, a_s.at[s, zz], a_r.at[xs, zz], dev(x, c, y, mir)).wait_recv()

    def gather_copy(s, up, ys, zz, frm, k):
        xs = (x + s) % 4
        blk = abuf.at[xs, ys * 2 + zz]
        to = (y + 1) % 4 if up else (y + 3) % 4
        return remote(blk, blk, g_s.at[s, k], g_r.at[s, frm, zz], dev(x, c, to, z))

    def gather_start(s):
        for k, (up, zz) in enumerate(((True, 0), (False, 1), (True, 1), (False, 0))):
            cp_ = gather_copy(s, up, y, zz, 0 if up else 1, k)
            cp_.start()
            sends.append(cp_)

    def gather_wait(s, frm, zz):
        ys = (y + (3, 1, 2)[frm]) % 4
        blk = abuf.at[(x + s) % 4, ys * 2 + zz]
        remote(blk, blk, g_s.at[s, 0], g_r.at[s, frm, zz], dev(x, c, y, mir)).wait_recv()

    def gather_forward(s):
        gather_wait(s, 0, 0)
        f1 = gather_copy(s, True, (y + 3) % 4, 0, 2, 4)
        f1.start()
        gather_wait(s, 1, 1)
        f2 = gather_copy(s, False, (y + 1) % 4, 1, 2, 5)
        f2.start()
        sends.extend((f1, f2))

    def gather_rest(s):
        gather_wait(s, 0, 1)
        gather_wait(s, 1, 0)
        gather_wait(s, 2, 0)
        gather_wait(s, 2, 1)

    def product(s, j, t):
        xs = (x + s) % 4
        rows = pl.ds(pl.multiple_of(t * 128, 128), 128)
        left = jnp.concatenate([abuf[xs, k, rows, :] for k in range(8)], axis=1)
        return jnp.dot(left, bbuf[j], preferred_element_type=jnp.float32)

    def partial_send(s):
        for j in range(2):
            @pl.loop(0, 3)
            def _(t):
                cp[s, j, pl.ds(pl.multiple_of(t * 128, 128), 128), :] = product(s, j, t)
            cp_ = remote(cp.at[s, j], cr.at[s, j], p_s.at[s, j], p_r.at[s, j], dev(x, c, y, buddy))
            cp_.start()
            sends.append(cp_)

    def finish(s):
        xd = (x + s) % 4
        h = x * 2 + par
        for j in (1, 0):
            remote(cp.at[s, j], cr.at[s, j], p_s.at[s, j], p_r.at[s, j], dev(x, c, y, buddy)).wait_recv()
            local = s == 0 and j == 0

            @pl.loop(0, 3)
            def _(t):
                rows = pl.ds(pl.multiple_of(t * 128, 128), 128)
                total = product(s, j + 2, t) + cr[s, j, rows, :]
                for q in range(2):
                    part = total[:, q * 128:(q + 1) * 128]
                    lines = pl.ds(t * 256 + q, 128, stride=2)
                    if local:
                        obuf[h, lines, :] = part
                    else:
                        cf[s, j, lines, :] = part
            if not local:
                zd = mir if j else z
                cp_ = remote(cf.at[s, j], obuf.at[h], o_s.at[s, j], o_r.at[h], dev(xd, c, y, zd))
                cp_.start()
                sends.append(cp_)

    a_start(0)
    b_start(0)
    b_start(1)
    a_start(1)
    b_start(2)
    b_start(3)
    a_start(2)
    a_start(3)
    a_arrive(0)
    gather_start(0)
    b_arrive(0)
    b_arrive(1)
    gather_forward(0)
    a_arrive(1)
    gather_start(1)
    b_arrive(2)
    b_arrive(3)
    for s in range(4):
        gather_rest(s)
        if s + 1 < 4:
            gather_forward(s + 1)
        if s + 2 < 4:
            a_arrive(s + 2)
            gather_start(s + 2)
        partial_send(s)
        if s:
            finish(s - 1)
    finish(3)

    for dx in range(4):
        for zz in range(2):
            xs = (x + dx) % 4
            h = xs * 2 + (par if zz == 0 else 1 - par)
            if dx or zz:
                remote(cf.at[0, 0], obuf.at[h], o_s.at[0, 0], o_r.at[h], dev(x, c, y, mir)).wait_recv()
            out[h] = res[h] + obuf[h]
    for cp_ in sends:
        cp_.wait_send()
    b_wait_sends()
    b_forward_wait()


def per_device(amp, integrals, residual_in):
    irreps, blocks, blk, kb, _ = integrals.shape
    rows = blocks * blk
    left = integrals.reshape(irreps, rows, kb * blk)
    right = amp.reshape(kb * blk, 16, 2 * blk).transpose(1, 0, 2)
    res = residual_in.reshape(irreps, rows * 2, blk)
    dma = pltpu.SemaphoreType.DMA
    out = pl.pallas_call(
        kernel,
        out_shape=jax.ShapeDtypeStruct(res.shape, jnp.float32),
        in_specs=[pl.BlockSpec(memory_space=pl.ANY), pl.BlockSpec(memory_space=pl.ANY), pl.BlockSpec(memory_space=pltpu.VMEM)],
        out_specs=pl.BlockSpec(memory_space=pltpu.VMEM),
        scratch_shapes=[
            pltpu.VMEM((4, 8, rows, 256), jnp.bfloat16),
            pltpu.VMEM((4, 2048, 256), jnp.bfloat16),
            pltpu.VMEM((4, 2, rows, 256), jnp.float32),
            pltpu.VMEM((4, 2, rows, 256), jnp.float32),
            pltpu.VMEM((4, 2, rows * 2, blk), jnp.float32),
            pltpu.VMEM((8, rows * 2, blk), jnp.float32),
            dma((4, 2)), dma((4, 2)),
            dma((4, 6)), dma((4, 3, 2)),
            dma((4, 4)), dma((4, 2, 4)), dma((4, 2, 4)),
            dma((4, 2)), dma((4, 2)),
            dma((4, 2)), dma((8,)),
        ],
        compiler_params=pltpu.CompilerParams(collective_id=0, has_side_effects=True, vmem_limit_bytes=60 << 20),
    )(left, right, res)
    return out.reshape(residual_in.shape)


def solution(mesh):
    placed = (
        P("row", "col", None, None, None),
        P(None, "row", None, "col", None),
        P(None, "row", None, "col", None),
    )
    return jax.shard_map(
        per_device,
        mesh=mesh,
        in_specs=placed,
        out_specs=P(None, "row", None, "col", None),
        check_vma=False,
    )
```

time: 387 us -> 166 us (0.43)
  the two profiles are of different devices: /device:TPU:3 before, /device:TPU:32 now
where the time goes in v1:
time: 166 us
  Pallas kernels  154 us (93%)
  local copies, waits for them, and re-layouts  12.3 us (7%)
    pallas_call x1, Pallas kernels, per_device(): pl.pallas_call(kernel, out_shape=jax.ShapeDtypeStruct(res.shape, jnp.floa...  154 us
    reshape x2, local copies, waits for them, and re-layouts, per_device(): right = amp.reshape(kb * blk, 16, 2 * blk).transpose(1, 0, 2)  4.7 us
    unnamed x1, local copies, waits for them, and re-layouts  3.86 us
    reshape x1, local copies, waits for them, and re-layouts, per_device(): left = integrals.reshape(irreps, rows, kb * blk)  3.73 us

profile of v1, /device:TPU:32, one launch (start us, length us, event | category | flops | bytes accessed | tf_op | source)
XLA Modules:
  0.0 166.0 jit_solution(3843078771107775640)
XLA Ops:
  0.0 3.7 %reshape.12.a_in = bf16[8,384,256]{2,1,0:T(8,128)(2,1)} reshape(bf16[8,3,128,2,128]{4,3,2,1,0:T(2,128)(2,1)} %param.4) | data formatting | bytes 3145728 | tf_op jit(solution)/shard_map/reshape | solution.py:244
  3.7 2.7 %reshape.13 = bf16[256,16,256]{2,1,0:T(8,128)(2,1)S(1)} reshape(bf16[1,2,128,32,128]{4,3,2,1,0:T(8,128)(2,1)} %param.3) | data formatting | bytes 4194304 | tf_op jit(solution)/shard_map/reshape | solution.py:245
  6.4 2.0 %copy.6 = bf16[256,16,256]{2,0,1:T(8,128)(2,1)} copy(bf16[256,16,256]{2,1,0:T(8,128)(2,1)S(1)} %reshape.13) | data formatting | bytes 4194304 | tf_op jit(solution)/shard_map/reshape | solution.py:245
  8.4 153.7 %shard_map.37 = f32[8,768,128]{2,1,0:T(8,128)} custom-call(bf16[8,384,256]{2,1,0:T(8,128)(2,1)} %reshape.12.a_in, bf16[16,256,256]{2,1,0:T(8,128)(2,1)} %bitcast.8, f32[8,768,128]{2,1,0:T(8,128)} %bitcast.9), custom_call_target="tpu_custom_call" | custom-call | tf_op jit(solution)/shard_map/pallas_call | solution.py:248
  162.1 3.9 %copy.8 = f32[8,3,128,2,128]{4,3,2,1,0:T(2,128)} copy(f32[8,3,128,2,128]{4,3,2,1,0:T(2,128)} %bitcast.7) | data formatting | bytes 6291456

commit v2 on v1

v2 whole, which is shorter than its diff:
```python
import jax
import jax.numpy as jnp
from jax import lax
from jax.experimental import pallas as pl
from jax.experimental.pallas import tpu as pltpu
from jax.sharding import PartitionSpec as P

MESH = pl.DeviceIdType.MESH
MODE = "full"
JXOR = (1, 2, 0, 3)
CHUNKS = ((0, 0), (1, 0), (1, 1), (2, 0), (2, 1), (3, 0), (3, 1), (0, 1))
NQ = len(CHUNKS)
LAG = 2
AHEAD = 2


def kernel(a_in, b_in, out, abuf, bbuf, cp, cr, cf,
           a_s, a_r, g_s, g_r, b_s, b_r, f_s, p_s, p_r, o_s, o_r):
    row, col = lax.axis_index("row"), lax.axis_index("col")
    x, c, y, z = row // 2, row % 2, col // 4, col % 4
    par = z // 2
    mir = 3 - z
    buddy = z + 1 - 2 * (z % 2)
    half = abuf.shape[2] // 2

    def dev(xx, cc, yy, zz):
        return (xx * 2 + cc, yy * 4 + zz)

    def xor(zz, j):
        lo, hi = zz % 2, zz // 2
        m = JXOR[j]
        lo = 1 - lo if m % 2 else lo
        hi = 1 - hi if m // 2 else hi
        return hi * 2 + lo

    def remote(src, dst, ss, rs, d):
        return pltpu.make_async_remote_copy(src, dst, ss, rs, device_id=d, device_id_type=MESH)

    barrier = pltpu.get_barrier_semaphore()
    peers = []
    for d in range(4):
        for zz in (z, mir):
            if d or zz is mir:
                peers.append(dev((x + d) % 4, c, y, zz))
            if d:
                peers.append(dev(x, c, (y + d) % 4, zz))
    peers.append(dev(x, 1 - c, y, z))
    peers.append(dev(x, c, y, buddy))
    for d in peers:
        pl.semaphore_signal(barrier, inc=1, device_id=d, device_id_type=MESH)
    pl.semaphore_wait(barrier, len(peers))

    sends = []

    def b_block(j, ys, zz):
        return bbuf.at[j, pl.ds(pl.multiple_of((ys * 2 + zz) * 256, 256), 256)]

    def b_start(j):
        for dy in (1, 3, 2, 0):
            yd = (y + dy) % 4

            def go(zd, zz, local):
                src = b_in.at[yd * 4 + xor(zd, j)]
                dst = b_block(j, y, zz)
                if local:
                    pltpu.make_async_copy(src, dst, b_r.at[y, zz, j]).start()
                else:
                    remote(src, dst, b_s.at[dy, j], b_r.at[y, zz, j], dev(x, c, yd, zd)).start()

            @pl.when(c == par)
            def _():
                go(z, 0, dy == 0)

            @pl.when(c != par)
            def _():
                go(mir, 1, False)

    def b_wait_sends():
        for j in range(4):
            for dy in range(4):
                cp_ = remote(b_in.at[0], b_block(0, 0, 0), b_s.at[dy, j], b_r.at[0, 0, j], dev(x, c, y, mir))
                if dy == 0:
                    @pl.when(c != par)
                    def _():
                        cp_.wait_send()
                else:
                    cp_.wait_send()

    def b_arrive(j):
        for dy in (0, 1, 3, 2):
            ys = (y + dy) % 4
            for zz in range(2):
                blk = b_block(j, ys, zz)
                fw = remote(blk, blk, f_s.at[dy, zz, j], b_r.at[ys, zz, j], dev(x, 1 - c, y, z))
                fw.wait_recv()

                @pl.when(c == par)
                def _():
                    fw.start()

    def b_forward_wait():
        @pl.when(c == par)
        def _():
            for j in range(4):
                for dy in range(4):
                    for zz in range(2):
                        blk = b_block(j, 0, 0)
                        remote(blk, blk, f_s.at[dy, zz, j], b_r.at[0, zz, j], dev(x, 1 - c, y, z)).wait_send()

    def a_copy(dx, r, zz):
        hx = (x + 4 - dx) % 4
        zd = mir if zz else z
        rows = pl.ds(r * half, half)
        src = a_in.at[hx * 2 + zd // 2, rows]
        dst = abuf.at[x, y * 2 + zz, rows]
        if dx == 0 and zz == 0:
            return pltpu.make_async_copy(src, dst, a_r.at[x, 0, r])
        return remote(src, dst, a_s.at[dx, zz, r], a_r.at[x, zz, r], dev(hx, c, y, zd))

    def a_start(q):
        dx, r = CHUNKS[q]
        for zz in (1, 0):
            cp_ = a_copy(dx, r, zz)
            cp_.start()
            if dx or zz:
                sends.append(cp_)

    def a_block(s, r, ys, zz):
        return abuf.at[(x + s) % 4, ys * 2 + zz, pl.ds(r * half, half)]

    def a_arrive(q):
        s, r = CHUNKS[q]
        for zz in range(2):
            if s == 0 and zz == 0:
                a_copy(0, r, 0).wait()
            else:
                blk = a_block(s, r, y, zz)
                remote(blk, blk, a_s.at[s, zz, r], a_r.at[(x + s) % 4, zz, r], dev(x, c, y, mir)).wait_recv()

    def gather_copy(q, up, ys, zz, frm, k):
        blk = a_block(*CHUNKS[q], ys, zz)
        to = (y + 1) % 4 if up else (y + 3) % 4
        return remote(blk, blk, g_s.at[q, k], g_r.at[q, frm, zz], dev(x, c, to, z))

    def gather_start(q):
        a_arrive(q)
        for k, (up, zz) in enumerate(((True, 0), (False, 1), (True, 1), (False, 0))):
            cp_ = gather_copy(q, up, y, zz, 0 if up else 1, k)
            cp_.start()
            sends.append(cp_)

    def gather_wait(q, frm, zz):
        blk = a_block(*CHUNKS[q], (y + (3, 1, 2)[frm]) % 4, zz)
        remote(blk, blk, g_s.at[q, 0], g_r.at[q, frm, zz], dev(x, c, y, mir)).wait_recv()

    def gather_forward(q):
        gather_wait(q, 0, 0)
        f1 = gather_copy(q, True, (y + 3) % 4, 0, 2, 4)
        f1.start()
        gather_wait(q, 1, 1)
        f2 = gather_copy(q, False, (y + 1) % 4, 1, 2, 5)
        f2.start()
        sends.extend((f1, f2))

    def gather_rest(q):
        gather_wait(q, 0, 1)
        gather_wait(q, 1, 0)
        gather_wait(q, 2, 0)
        gather_wait(q, 2, 1)

    def product(q, j, dst):
        s, r = CHUNKS[q]
        left = jnp.concatenate([abuf[(x + s) % 4, k, pl.ds(r * half, half), :] for k in range(8)], axis=1)
        total = jnp.dot(left, bbuf[j], preferred_element_type=jnp.float32)
        for i in range(2):
            dst[pl.ds(i, half, stride=2), :] = total[:, i * 128:(i + 1) * 128]

    def partial_copy(q, j):
        return remote(cp.at[q, j], cr.at[q, j], p_s.at[q, j], p_r.at[q, j], dev(x, c, y, buddy))

    def partial_send(q):
        @pl.loop(0, 2)
        def _(j):
            product(q, j, cp.at[q, j])
            partial_copy(q, j).start()

    def final_copy(q, j):
        s, r = CHUNKS[q]
        lines = pl.ds(r * 2 * half, 2 * half)
        h = x * 2 + par
        dst = out.at[h, lines]
        if s == 0 and j == 0:
            return pltpu.make_async_copy(cf.at[q, j], dst, o_s.at[q, j])
        return remote(cf.at[q, j], dst, o_s.at[q, j], o_r.at[h, r], dev((x + s) % 4, c, y, mir if j else z))

    def finish(q):
        @pl.loop(0, 2)
        def _(j):
            product(q, j + 2, cf.at[q, j])

        for j in (1, 0):
            partial_copy(q, j).wait_recv()
            cf[q, j] += cr[q, j]
            final_copy(q, j).start()

    a_start(0)
    b_start(0)
    b_start(1)
    a_start(1)
    a_start(2)
    gather_start(0)
    b_arrive(0)
    gather_forward(0)
    a_start(3)
    gather_start(1)
    b_arrive(1)
    for q in range(NQ):
        if q + 4 < NQ:
            a_start(q + 4)
        if q + 2 < NQ:
            gather_start(q + 2)
        if q == 0:
            b_start(2)
            b_start(3)
        if q + 1 < NQ:
            gather_forward(q + 1)
        gather_rest(q)
        partial_send(q)
        if q == LAG - 1:
            b_arrive(2)
            b_arrive(3)
        if q >= LAG:
            finish(q - LAG)
    for q in range(NQ - LAG, NQ):
        finish(q)

    for q in range(NQ):
        for j in range(2):
            partial_copy(q, j).wait_send()
            s, r = CHUNKS[q]
            if s == 0 and j == 0:
                final_copy(q, j).wait()
            else:
                final_copy(q, j).wait_send()
                h = (x + 4 - s) % 4 * 2 + (1 - par if j else par)
                dst = out.at[h, pl.ds(r * 2 * half, 2 * half)]
                remote(cf.at[q, j], dst, o_s.at[q, j], o_r.at[h, r], dev(x, c, y, mir)).wait_recv()
    for cp_ in sends:
        cp_.wait_send()
    b_wait_sends()
    b_forward_wait()


def per_device(amp, integrals, residual_in):
    irreps, blocks, blk, kb, _ = integrals.shape
    rows = blocks * blk
    left = integrals.reshape(irreps, rows, kb * blk)
    right = amp.reshape(kb * blk, 16, 2 * blk).transpose(1, 0, 2)
    dma = pltpu.SemaphoreType.DMA
    out = pl.pallas_call(
        kernel,
        out_shape=jax.ShapeDtypeStruct((irreps, rows * 2, blk), jnp.float32),
        in_specs=[pl.BlockSpec(memory_space=pl.ANY)] * 2,
        out_specs=pl.BlockSpec(memory_space=pl.ANY),
        scratch_shapes=[
            pltpu.VMEM((4, 8, rows, 256), jnp.bfloat16),
            pltpu.VMEM((4, 2048, 256), jnp.bfloat16),
            pltpu.VMEM((NQ, 2, rows, blk), jnp.float32),
            pltpu.VMEM((NQ, 2, rows, blk), jnp.float32),
            pltpu.VMEM((NQ, 2, rows, blk), jnp.float32),
            dma((4, 2, 2)), dma((4, 2, 2)),
            dma((NQ, 6)), dma((NQ, 3, 2)),
            dma((4, 4)), dma((4, 2, 4)), dma((4, 2, 4)),
            dma((NQ, 2)), dma((NQ, 2)),
            dma((NQ, 2)), dma((8, 2)),
        ],
        compiler_params=pltpu.CompilerParams(collective_id=0, has_side_effects=True, vmem_limit_bytes=60 << 20),
    )(left, right)
    return residual_in + out.reshape(residual_in.shape)


def solution(mesh):
    placed = (
        P("row", "col", None, None, None),
        P(None, "row", None, "col", None),
        P(None, "row", None, "col", None),
    )
    return jax.shard_map(
        per_device,
        mesh=mesh,
        in_specs=placed,
        out_specs=P(None, "row", None, "col", None),
        check_vma=False,
    )
```

time: 166 us -> 136 us (0.82)
  the two profiles are of different devices: /device:TPU:32 before, /device:TPU:3 now
where the time goes in v2:
time: 136 us; the launch traced here: 134 us
  Pallas kernels  120 us (88%)
  local copies, waits for them, and re-layouts  8.43 us (6%)
  other arithmetic  5.62 us (4%)
    pallas_call x1, Pallas kernels, per_device(): pl.pallas_call(kernel, out_shape=jax.ShapeDtypeStruct((irreps, rows * 2,...  120 us
    add x1, other arithmetic, per_device(): return residual_in + out.reshape(residual_in.shape)  5.62 us
    reshape x2, local copies, waits for them, and re-layouts, per_device(): right = amp.reshape(kb * blk, 16, 2 * blk).transpose(1, 0, 2)  4.7 us
    reshape x1, local copies, waits for them, and re-layouts, per_device(): left = integrals.reshape(irreps, rows, kb * blk)  3.73 us

profile of v2, /device:TPU:3, one launch (start us, length us, event | category | flops | bytes accessed | tf_op | source)
XLA Modules:
  0.0 133.7 jit_solution(9963293791407770940)
XLA Ops:
  0.0 3.7 %reshape.9.a_in = bf16[8,384,256]{2,1,0:T(8,128)(2,1)} reshape(bf16[8,3,128,2,128]{4,3,2,1,0:T(2,128)(2,1)} %param.4) | data formatting | bytes 3145728 | tf_op jit(solution)/shard_map/reshape | solution.py:257
  3.7 2.7 %reshape.10 = bf16[256,16,256]{2,1,0:T(8,128)(2,1)S(1)} reshape(bf16[1,2,128,32,128]{4,3,2,1,0:T(8,128)(2,1)} %param.3) | data formatting | bytes 4194304 | tf_op jit(solution)/shard_map/reshape | solution.py:258
  6.4 2.0 %copy.6 = bf16[256,16,256]{2,0,1:T(8,128)(2,1)} copy(bf16[256,16,256]{2,1,0:T(8,128)(2,1)S(1)} %reshape.10) | data formatting | bytes 4194304 | tf_op jit(solution)/shard_map/reshape | solution.py:258
  8.4 0.0 copy-start
  8.4 119.6 %shard_map.37 = f32[8,768,128]{2,1,0:T(8,128)} custom-call(bf16[8,384,256]{2,1,0:T(8,128)(2,1)} %reshape.9.a_in, bf16[16,256,256]{2,1,0:T(8,128)(2,1)} %bitcast.7), custom_call_target="tpu_custom_call" | custom-call | tf_op jit(solution)/shard_map/pallas_call | solution.py:260
  128.1 0.0 copy-done
  128.1 5.6 %add.3 = f32[8,3,128,2,128]{4,3,2,1,0:T(2,128)} add(f32[8,3,128,2,128]{4,3,2,1,0:T(2,128)S(1)} %copy-done, f32[8,3,128,2,128]{4,3,2,1,0:T(2,128)} %bitcast.6) | non-fusion elementwise | flops 786432 | bytes 9437184 | tf_op jit(solution)/shard_map/add | solution.py:279
Async XLA Ops:
  8.4 119.6 %copy-start = (f32[8,3,128,2,128]{4,3,2,1,0:T(2,128)S(1)}, f32[8,3,128,2,128]{4,3,2,1,0:T(2,128)}, u32[]{:S(2)}) copy-start(f32[8,3,128,2,128]{4,3,2,1,0:T(2,128)} %param.5) | copy-start | bytes 9437188

commit v3 on v2

v3 whole, which is shorter than its diff:
```python
import jax
import jax.numpy as jnp
from jax import lax
from jax.experimental import pallas as pl
from jax.experimental.pallas import tpu as pltpu
from jax.sharding import PartitionSpec as P

MESH = pl.DeviceIdType.MESH
JXOR = (1, 2, 0, 3)
CHUNKS = (
    (0, 0, 192), (1, 0, 192), (1, 192, 192), (2, 0, 192), (2, 192, 192),
    (3, 0, 192), (3, 192, 192), (0, 192, 192),
)
NQ = len(CHUNKS)
BASE = tuple(2 * sum(n for _, _, n in CHUNKS[:q]) for q in range(NQ))
LINES = 2 * sum(n for _, _, n in CHUNKS)
PLAN = (
    "AS0", "BS1", "BL0", "BS0", "AS1", "GS0", "AS2", "BA1", "GF0", "AS3", "GS1", "BA0", "BL2", "BL3", "AS4",
    "GS2", "BS3", "BS2", "GF1", "GR0", "P0", "AS5", "GS3", "GF2", "GR1", "P1", "BA3", "BA2", "AS6", "GS4", "GF3",
    "GR2", "P2", "F0", "AS7", "GS5", "GF4", "GR3", "P3", "F1", "GS6", "GF5", "GR4", "P4", "F2", "GS7", "GF6",
    "GR5", "P5", "F3", "GF7", "GR6", "P6", "F4", "GR7", "P7", "F5", "O60", "O61", "O70", "O71", "W61", "W60",
    "W71", "W70",
)


def kernel(a_in, b_in, out, araw, braw, atmp, btmp, ast, bst, abuf, bbuf, cp, cr, cf,
           in_s, a_s, a_r, g_s, g_r, b_s, b_r, f_s, p_s, p_r, o_s, o_r):
    row, col = lax.axis_index("row"), lax.axis_index("col")
    x, c, y, z = row // 2, row % 2, col // 4, col % 4
    par = z // 2
    mir = 3 - z
    buddy = z + 1 - 2 * (z % 2)

    def dev(xx, cc, yy, zz):
        return (xx * 2 + cc, yy * 4 + zz)

    def xor(zz, j):
        lo, hi = zz % 2, zz // 2
        m = JXOR[j]
        lo = 1 - lo if m % 2 else lo
        hi = 1 - hi if m // 2 else hi
        return hi * 2 + lo

    def remote(src, dst, ss, rs, d):
        return pltpu.make_async_remote_copy(src, dst, ss, rs, device_id=d, device_id_type=MESH)

    b_load = pltpu.make_async_copy(b_in, braw, in_s.at[0])
    a_load = pltpu.make_async_copy(a_in, araw, in_s.at[1])
    b_load.start()
    a_load.start()
    barrier = pltpu.get_barrier_semaphore()
    peers = []
    for d in range(4):
        for zz in (z, mir):
            if d or zz is mir:
                peers.append(dev((x + d) % 4, c, y, zz))
            if d:
                peers.append(dev(x, c, (y + d) % 4, zz))
    peers.append(dev(x, 1 - c, y, z))
    peers.append(dev(x, c, y, buddy))
    for d in peers:
        pl.semaphore_signal(barrier, inc=1, device_id=d, device_id_type=MESH)
    b_load.wait()

    @pl.loop(0, 8)
    def _(t):
        ks = pl.ds(t * 32, 32)
        btmp[pl.ds(t * 1024, 1024), :] = braw[ks].astype(jnp.float32).reshape(1024, 128)

    def b_lay(j):
        zj = jnp.where(c == par, xor(z, j), xor(mir, j))
        for yd in range(4):
            for i in range(2):
                lines = btmp[pl.ds(yd * 8 + zj * 2 + i, 256, stride=32), :]
                bst[j, yd, :, i * 128:(i + 1) * 128] = lines.astype(jnp.bfloat16)

    def a_lay(q):
        dx, off, n = CHUNKS[q]
        hx = (x + 4 - dx) % 4
        for zz in range(2):
            h = hx * 2 + (1 - par if zz else par)
            atmp[pl.ds(0, 2 * n), :] = araw[h, pl.ds(2 * off, 2 * n), :].astype(jnp.float32)
            for i in range(2):
                lines = atmp[pl.ds(i, n, stride=2), :].astype(jnp.bfloat16)
                lanes = slice(i * 128, (i + 1) * 128)
                if dx == 0 and zz == 0:
                    abuf[x, y * 2, off:off + n, lanes] = lines
                else:
                    ast[h, off:off + n, lanes] = lines

    b_lay(1)
    a_load.wait()
    a_lay(0)
    pl.semaphore_wait(barrier, len(peers))

    sends = []

    def b_block(j, ys, zz):
        return bbuf.at[j, pl.ds(pl.multiple_of((ys * 2 + zz) * 256, 256), 256)]

    def b_start(j, dys=(1, 3, 2, 0)):
        for dy in dys:
            yd = (y + dy) % 4

            def go(zd, zz, local):
                src = bst.at[j, yd]
                dst = b_block(j, y, zz)
                if local:
                    pltpu.make_async_copy(src, dst, b_r.at[y, zz, j]).start()
                else:
                    remote(src, dst, b_s.at[dy, j], b_r.at[y, zz, j], dev(x, c, yd, zd)).start()

            @pl.when(c == par)
            def _():
                go(z, 0, dy == 0)

            @pl.when(c != par)
            def _():
                go(mir, 1, False)

    def b_wait_sends():
        for j in range(4):
            for dy in range(4):
                cp_ = remote(bst.at[0, 0], b_block(0, 0, 0), b_s.at[dy, j], b_r.at[0, 0, j], dev(x, c, y, mir))
                if dy == 0:
                    @pl.when(c != par)
                    def _():
                        cp_.wait_send()
                else:
                    cp_.wait_send()

    def b_arrive(j):
        for dy in (0, 1, 3, 2):
            ys = (y + dy) % 4
            for zz in range(2):
                blk = b_block(j, ys, zz)
                fw = remote(blk, blk, f_s.at[dy, zz, j], b_r.at[ys, zz, j], dev(x, 1 - c, y, z))
                fw.wait_recv()

                @pl.when(c == par)
                def _():
                    fw.start()

    def b_forward_wait():
        @pl.when(c == par)
        def _():
            for j in range(4):
                for dy in range(4):
                    for zz in range(2):
                        blk = b_block(j, 0, 0)
                        remote(blk, blk, f_s.at[dy, zz, j], b_r.at[0, zz, j], dev(x, 1 - c, y, z)).wait_send()

    def a_block(q, ys, zz):
        s, off, n = CHUNKS[q]
        return abuf.at[(x + s) % 4, ys * 2 + zz, pl.ds(off, n)]

    def a_start(q):
        dx, off, n = CHUNKS[q]
        hx = (x + 4 - dx) % 4
        if q:
            a_lay(q)
        for zz in (1, 0):
            if dx or zz:
                zd = mir if zz else z
                src = ast.at[hx * 2 + zd // 2, pl.ds(off, n)]
                dst = abuf.at[x, y * 2 + zz, pl.ds(off, n)]
                cp_ = remote(src, dst, a_s.at[q, zz], a_r.at[q, zz], dev(hx, c, y, zd))
                cp_.start()
                sends.append(cp_)

    def a_arrive(q, zz):
        if CHUNKS[q][0] or zz:
            blk = a_block(q, y, zz)
            remote(blk, blk, a_s.at[q, zz], a_r.at[q, zz], dev(x, c, y, mir)).wait_recv()

    def gather_copy(q, up, ys, zz, frm, k):
        blk = a_block(q, ys, zz)
        to = (y + 1) % 4 if up else (y + 3) % 4
        return remote(blk, blk, g_s.at[q, k], g_r.at[q, frm, zz], dev(x, c, to, z))

    def gather_start(q):
        for k, (up, zz) in enumerate(((True, 0), (False, 0), (False, 1), (True, 1))):
            if k == 0 or k == 2:
                a_arrive(q, zz)
            cp_ = gather_copy(q, up, y, zz, 0 if up else 1, k)
            cp_.start()
            sends.append(cp_)

    def gather_wait(q, frm, zz):
        blk = a_block(q, (y + (3, 1, 2)[frm]) % 4, zz)
        remote(blk, blk, g_s.at[q, 0], g_r.at[q, frm, zz], dev(x, c, y, mir)).wait_recv()

    def gather_forward(q):
        gather_wait(q, 0, 0)
        f1 = gather_copy(q, True, (y + 3) % 4, 0, 2, 4)
        f1.start()
        gather_wait(q, 1, 1)
        f2 = gather_copy(q, False, (y + 1) % 4, 1, 2, 5)
        f2.start()
        sends.extend((f1, f2))

    def gather_rest(q):
        gather_wait(q, 0, 1)
        gather_wait(q, 1, 0)
        gather_wait(q, 2, 0)
        gather_wait(q, 2, 1)

    def product(q, j, dst):
        s, off, n = CHUNKS[q]
        left = jnp.concatenate([abuf[(x + s) % 4, k, pl.ds(off, n), :] for k in range(8)], axis=1)
        total = jnp.dot(left, bbuf[j], preferred_element_type=jnp.float32)
        for i in range(2):
            dst[pl.ds(BASE[q] + i, n, stride=2), :] = total[:, i * 128:(i + 1) * 128]

    def lines_of(q):
        return pl.ds(BASE[q], 2 * CHUNKS[q][2])

    def partial_copy(q, j):
        return remote(cp.at[j, lines_of(q)], cr.at[j, lines_of(q)], p_s.at[q, j], p_r.at[q, j], dev(x, c, y, buddy))

    def partial_send(q, first=0, count=2):
        @pl.loop(first, first + count)
        def _(i):
            j = 1 - i
            product(q, j, cp.at[j])
            partial_copy(q, j).start()

    def final_copy(q, j):
        s, off, n = CHUNKS[q]
        src = cf.at[j, lines_of(q)]
        dst = out.at[x * 2 + par, pl.ds(2 * off, 2 * n)]
        if s == 0 and j == 0:
            return pltpu.make_async_copy(src, dst, o_s.at[q, j])
        return remote(src, dst, o_s.at[q, j], o_r.at[q, j], dev((x + s) % 4, c, y, mir if j else z))

    def final_arrive(q, j):
        s, off, n = CHUNKS[q]
        h = (x + 4 - s) % 4 * 2 + (1 - par if j else par)
        dst = out.at[h, pl.ds(2 * off, 2 * n)]
        remote(cf.at[j, lines_of(q)], dst, o_s.at[q, j], o_r.at[q, j], dev(x, c, y, mir)).wait_recv()

    def own(q, j):
        product(q, j + 2, cf.at[j])

    def finish(q, j):
        partial_copy(q, j).wait_recv()
        cf[j, lines_of(q), :] += cr[j, lines_of(q), :]
        final_copy(q, j).start()

    steps = dict(AS=a_start, BL=b_lay, BA=b_arrive, GS=gather_start, GF=gather_forward, GR=gather_rest)
    for step in PLAN:
        args = [int(d) for d in step if d.isdigit()]
        name = step.rstrip("0123456789")
        if name == "P":
            partial_send(args[0], *((1 - args[1], 1) if len(args) > 1 else ()))
        elif name == "BS":
            b_start(args[0], ((1, 3), (2, 0))[args[1]] if len(args) > 1 else (1, 3, 2, 0))
        elif name == "F":
            for j in args[1:] or (1, 0):
                own(args[0], j)
                finish(args[0], j)
        elif name == "O":
            own(*args)
        elif name == "W":
            finish(*args)
        else:
            steps[name](*args)

    for q in range(NQ):
        for j in range(2):
            partial_copy(q, j).wait_send()
            if CHUNKS[q][0] == 0 and j == 0:
                final_copy(q, j).wait()
            else:
                final_copy(q, j).wait_send()
                final_arrive(q, j)
    for cp_ in sends:
        cp_.wait_send()
    b_wait_sends()
    b_forward_wait()


def per_device(amp, integrals, residual_in):
    irreps, blocks, blk, kb, _ = integrals.shape
    rows = blocks * blk
    left = integrals.reshape(irreps, rows * kb, blk)
    right = amp.reshape(kb * blk, 32, blk)
    res = residual_in.reshape(irreps, rows * 2, blk)
    dma = pltpu.SemaphoreType.DMA
    out = pl.pallas_call(
        kernel,
        out_shape=jax.ShapeDtypeStruct(res.shape, jnp.float32),
        in_specs=[pl.BlockSpec(memory_space=pl.ANY)] * 2,
        out_specs=pl.BlockSpec(memory_space=pl.ANY),
        scratch_shapes=[
            pltpu.VMEM(left.shape, jnp.bfloat16),
            pltpu.VMEM(right.shape, jnp.bfloat16),
            pltpu.VMEM((384, blk), jnp.float32),
            pltpu.VMEM((8192, blk), jnp.float32),
            pltpu.VMEM((8, rows, 256), jnp.bfloat16),
            pltpu.VMEM((4, 4, 256, 256), jnp.bfloat16),
            pltpu.VMEM((4, 8, rows, 256), jnp.bfloat16),
            pltpu.VMEM((4, 2048, 256), jnp.bfloat16),
            pltpu.VMEM((2, LINES, blk), jnp.float32),
            pltpu.VMEM((2, LINES, blk), jnp.float32),
            pltpu.VMEM((2, LINES, blk), jnp.float32),
            dma((2,)),
            dma((NQ, 2)), dma((NQ, 2)),
            dma((NQ, 6)), dma((NQ, 3, 2)),
            dma((4, 4)), dma((4, 2, 4)), dma((4, 2, 4)),
            dma((NQ, 2)), dma((NQ, 2)),
            dma((NQ, 2)), dma((NQ, 2)),
        ],
        compiler_params=pltpu.CompilerParams(collective_id=0, has_side_effects=True, vmem_limit_bytes=60 << 20),
    )(left, right)
    return (res + out).reshape(residual_in.shape)


def solution(mesh):
    placed = (
        P("row", "col", None, None, None),
        P(None, "row", None, "col", None),
        P(None, "row", None, "col", None),
    )
    return jax.shard_map(
        per_device,
        mesh=mesh,
        in_specs=placed,
        out_specs=P(None, "row", None, "col", None),
        check_vma=False,
    )
```

time: 136 us -> 123 us (0.904); the launches traced: 134 us -> 122 us
  local copies, waits for them, and re-layouts: 8.43 us -> 0.01 us
  other arithmetic: 5.62 us -> 3.87 us
    reshape x3 -> x0, local copies, waits for them, and re-layouts: 8.43 us -> none  [the longest x2 4.7 us: per_device(): right = amp.reshape(kb * blk, 16, 2 * blk).transpose(1, 0, 2)]
    add x1, other arithmetic: 5.62 us -> 3.87 us  [per_device(): return (res + out).reshape(residual_in.shape)]
where the time goes in v3:
time: 123 us; the launch traced here: 122 us
  Pallas kernels  119 us (97%)
  other arithmetic  3.87 us (3%)
    pallas_call x1, Pallas kernels, per_device(): pl.pallas_call(kernel, out_shape=jax.ShapeDtypeStruct(res.shape, jnp.floa...  119 us
    add x1, other arithmetic, per_device(): return (res + out).reshape(residual_in.shape)  3.87 us

profile of v3, /device:TPU:3, one launch (start us, length us, event | category | flops | bytes accessed | tf_op | source)
XLA Modules:
  0.0 122.4 jit_solution(11738969210487021215)
XLA Ops:
  0.0 0.0 copy-start
  0.0 118.5 %shard_map.37 = f32[8,768,128]{2,1,0:T(8,128)} custom-call(bf16[8,768,128]{2,1,0:T(8,128)(2,1)} %bitcast.6, bf16[256,32,128]{2,1,0:T(8,128)(2,1)} %bitcast.5), custom_call_target="tpu_custom_call" | custom-call | tf_op jit(solution)/shard_map/pallas_call | solution.py:290
  118.5 0.0 copy-done
  118.5 3.9 %add.3 = f32[8,768,128]{2,1,0:T(8,128)} add(f32[8,768,128]{2,1,0:T(8,128)S(1)} %bitcast.4, f32[8,768,128]{2,1,0:T(8,128)} %shard_map.37) | non-fusion elementwise | flops 786432 | bytes 9437184 | tf_op jit(solution)/shard_map/add | solution.py:316
Async XLA Ops:
  0.0 118.5 %copy-start = (f32[8,3,128,2,128]{4,3,2,1,0:T(2,128)S(1)}, f32[8,3,128,2,128]{4,3,2,1,0:T(2,128)}, u32[]{:S(2)}) copy-start(f32[8,3,128,2,128]{4,3,2,1,0:T(2,128)} %param.5) | copy-start | bytes 9437188

commit v4 on v3

--- a/solution.py
+++ b/solution.py
@@ -14,12 +14,13 @@
 NQ = len(CHUNKS)
 BASE = tuple(2 * sum(n for _, _, n in CHUNKS[:q]) for q in range(NQ))
 LINES = 2 * sum(n for _, _, n in CHUNKS)
+PIECES = (4, 1, 1, 2)
 PLAN = (
-    "AS0", "BS1", "BL0", "BS0", "AS1", "GS0", "AS2", "BA1", "GF0", "AS3", "GS1", "BA0", "BL2", "BL3", "AS4",
-    "GS2", "BS3", "BS2", "GF1", "GR0", "P0", "AS5", "GS3", "GF2", "GR1", "P1", "BA3", "BA2", "AS6", "GS4", "GF3",
-    "GR2", "P2", "F0", "AS7", "GS5", "GF4", "GR3", "P3", "F1", "GS6", "GF5", "GR4", "P4", "F2", "GS7", "GF6",
-    "GR5", "P5", "F3", "GF7", "GR6", "P6", "F4", "GR7", "P7", "F5", "O60", "O61", "O70", "O71", "W61", "W60",
-    "W71", "W70",
+    "AS0", "BS1", "BL0", "BS0", "AS1", "GS0", "AS2", "BA1", "GF0", "AS3", "GS1", "BL2", "BL3", "GR0", "P01",
+    "BA0", "AS4", "GS2", "GF1", "P00", "AS5", "GS3", "BS3", "BS2", "GF2", "GR1", "P1", "AS6", "GS4", "GF3", "GR2",
+    "P2", "BA3", "BA2", "F01", "F00", "AS7", "GS5", "GF4", "GR3", "P3", "F11", "F10", "GS6", "GF5", "GR4", "P4",
+    "F21", "F20", "GS7", "GF6", "GR5", "P5", "F31", "F30", "GF7", "GR6", "P6", "F41", "F40", "GR7", "P7", "F51",
+    "F50", "O61", "O60", "O71", "O70", "Z", "W61", "W60", "W71", "W70",
 )
 
 
@@ -95,6 +96,14 @@
 
     sends = []
 
+    def start(blocks, pieces):
+        src, dst, off, n, ss, rs, d = blocks
+        for k in range(pieces):
+            rows = pl.ds(off + k * (n // pieces), n // pieces)
+            remote(src.at[rows], dst.at[rows], ss, rs, d).start()
+        rows = pl.ds(off, n)
+        sends.append(remote(src.at[rows], dst.at[rows], ss, rs, d))
+
     def b_block(j, ys, zz):
         return bbuf.at[j, pl.ds(pl.multiple_of((ys * 2 + zz) * 256, 256), 256)]
 
@@ -129,26 +138,32 @@
                 else:
                     cp_.wait_send()
 
+    def b_pair(j, dy):
+        ys = (y + dy) % 4
+        blk = bbuf.at[j, pl.ds(pl.multiple_of(ys * 512, 512), 512)]
+        return remote(blk, blk, f_s.at[dy, j], b_r.at[ys, 0, j], dev(x, 1 - c, y, z))
+
     def b_arrive(j):
         for dy in (0, 1, 3, 2):
             ys = (y + dy) % 4
-            for zz in range(2):
-                blk = b_block(j, ys, zz)
-                fw = remote(blk, blk, f_s.at[dy, zz, j], b_r.at[ys, zz, j], dev(x, 1 - c, y, z))
-                fw.wait_recv()
-
-                @pl.when(c == par)
-                def _():
-                    fw.start()
+
+            @pl.when(c == par)
+            def _():
+                for zz in range(2):
+                    blk = b_block(j, ys, zz)
+                    remote(blk, blk, f_s.at[dy, j], b_r.at[ys, zz, j], dev(x, 1 - c, y, z)).wait_recv()
+                b_pair(j, dy).start()
+
+            @pl.when(c != par)
+            def _():
+                b_pair(j, dy).wait_recv()
 
     def b_forward_wait():
         @pl.when(c == par)
         def _():
             for j in range(4):
                 for dy in range(4):
-                    for zz in range(2):
-                        blk = b_block(j, 0, 0)
-                        remote(blk, blk, f_s.at[dy, zz, j], b_r.at[0, zz, j], dev(x, 1 - c, y, z)).wait_send()
+                    b_pair(j, dy).wait_send()
 
     def a_block(q, ys, zz):
         s, off, n = CHUNKS[q]
@@ -162,29 +177,25 @@
         for zz in (1, 0):
             if dx or zz:
                 zd = mir if zz else z
-                src = ast.at[hx * 2 + zd // 2, pl.ds(off, n)]
-                dst = abuf.at[x, y * 2 + zz, pl.ds(off, n)]
-                cp_ = remote(src, dst, a_s.at[q, zz], a_r.at[q, zz], dev(hx, c, y, zd))
-                cp_.start()
-                sends.append(cp_)
+                start((ast.at[hx * 2 + zd // 2], abuf.at[x, y * 2 + zz], off, n,
+                       a_s.at[q, zz], a_r.at[q, zz], dev(hx, c, y, zd)), PIECES[0] if q == 0 else PIECES[1])
 
     def a_arrive(q, zz):
         if CHUNKS[q][0] or zz:
             blk = a_block(q, y, zz)
             remote(blk, blk, a_s.at[q, zz], a_r.at[q, zz], dev(x, c, y, mir)).wait_recv()
 
-    def gather_copy(q, up, ys, zz, frm, k):
-        blk = a_block(q, ys, zz)
+    def gather_copy(q, up, ys, zz, frm, k, pieces):
+        s, off, n = CHUNKS[q]
+        blk = abuf.at[(x + s) % 4, ys * 2 + zz]
         to = (y + 1) % 4 if up else (y + 3) % 4
-        return remote(blk, blk, g_s.at[q, k], g_r.at[q, frm, zz], dev(x, c, to, z))
+        start((blk, blk, off, n, g_s.at[q, k], g_r.at[q, frm, zz], dev(x, c, to, z)), pieces)
 
     def gather_start(q):
         for k, (up, zz) in enumerate(((True, 0), (False, 0), (False, 1), (True, 1))):
             if k == 0 or k == 2:
                 a_arrive(q, zz)
-            cp_ = gather_copy(q, up, y, zz, 0 if up else 1, k)
-            cp_.start()
-            sends.append(cp_)
+            gather_copy(q, up, y, zz, 0 if up else 1, k, PIECES[2])
 
     def gather_wait(q, frm, zz):
         blk = a_block(q, (y + (3, 1, 2)[frm]) % 4, zz)
@@ -192,12 +203,9 @@
 
     def gather_forward(q):
         gather_wait(q, 0, 0)
-        f1 = gather_copy(q, True, (y + 3) % 4, 0, 2, 4)
-        f1.start()
+        gather_copy(q, True, (y + 3) % 4, 0, 2, 4, PIECES[3])
         gather_wait(q, 1, 1)
-        f2 = gather_copy(q, False, (y + 1) % 4, 1, 2, 5)
-        f2.start()
-        sends.extend((f1, f2))
+        gather_copy(q, False, (y + 1) % 4, 1, 2, 5, PIECES[3])
 
     def gather_rest(q):
         gather_wait(q, 0, 1)
@@ -205,12 +213,14 @@
         gather_wait(q, 2, 0)
         gather_wait(q, 2, 1)
 
-    def product(q, j, dst):
+    def product(q, j, dst, more=None):
         s, off, n = CHUNKS[q]
         left = jnp.concatenate([abuf[(x + s) % 4, k, pl.ds(off, n), :] for k in range(8)], axis=1)
         total = jnp.dot(left, bbuf[j], preferred_element_type=jnp.float32)
         for i in range(2):
-            dst[pl.ds(BASE[q] + i, n, stride=2), :] = total[:, i * 128:(i + 1) * 128]
+            lines = pl.ds(BASE[q] + i, n, stride=2)
+            part = total[:, i * 128:(i + 1) * 128]
+            dst[lines, :] = part if more is None else part + more[lines, :]
 
     def lines_of(q):
         return pl.ds(BASE[q], 2 * CHUNKS[q][2])
@@ -257,8 +267,14 @@
             b_start(args[0], ((1, 3), (2, 0))[args[1]] if len(args) > 1 else (1, 3, 2, 0))
         elif name == "F":
             for j in args[1:] or (1, 0):
-                own(args[0], j)
-                finish(args[0], j)
+                partial_copy(args[0], j).wait_recv()
+                product(args[0], j + 2, cf.at[j], cr.at[j])
+                final_copy(args[0], j).start()
+        elif name == "Z":
+            for cp_ in sends:
+                cp_.wait_send()
+            b_wait_sends()
+            b_forward_wait()
         elif name == "O":
             own(*args)
         elif name == "W":
@@ -274,11 +290,6 @@
             else:
                 final_copy(q, j).wait_send()
                 final_arrive(q, j)
-    for cp_ in sends:
-        cp_.wait_send()
-    b_wait_sends()
-    b_forward_wait()
-
 
 def per_device(amp, integrals, residual_in):
     irreps, blocks, blk, kb, _ = integrals.shape
@@ -307,7 +318,7 @@
             dma((2,)),
             dma((NQ, 2)), dma((NQ, 2)),
             dma((NQ, 6)), dma((NQ, 3, 2)),
-            dma((4, 4)), dma((4, 2, 4)), dma((4, 2, 4)),
+            dma((4, 4)), dma((4, 2, 4)), dma((4, 4)),
             dma((NQ, 2)), dma((NQ, 2)),
             dma((NQ, 2)), dma((NQ, 2)),
         ],

time: 123 us -> 123 us (level)
  no operation moved by 1% of the time
where the time goes in v4:
time: 123 us; the launch traced here: 122 us
  Pallas kernels  119 us (97%)
  other arithmetic  3.87 us (3%)
    pallas_call x1, Pallas kernels, per_device(): pl.pallas_call(kernel, out_shape=jax.ShapeDtypeStruct(res.shape, jnp.floa...  119 us
    add x1, other arithmetic, per_device(): return (res + out).reshape(residual_in.shape)  3.87 us

profile of v4, /device:TPU:3, one launch (start us, length us, event | category | flops | bytes accessed | tf_op | source)
XLA Modules:
  0.0 122.5 jit_solution(14488544927620456772)
XLA Ops:
  0.0 0.0 copy-start
  0.0 118.6 %shard_map.37 = f32[8,768,128]{2,1,0:T(8,128)} custom-call(bf16[8,768,128]{2,1,0:T(8,128)(2,1)} %bitcast.6, bf16[256,32,128]{2,1,0:T(8,128)(2,1)} %bitcast.5), custom_call_target="tpu_custom_call" | custom-call | tf_op jit(solution)/shard_map/pallas_call | solution.py:301
  118.6 0.0 copy-done
  118.6 3.9 %add.3 = f32[8,768,128]{2,1,0:T(8,128)} add(f32[8,768,128]{2,1,0:T(8,128)S(1)} %bitcast.4, f32[8,768,128]{2,1,0:T(8,128)} %shard_map.37) | non-fusion elementwise | flops 786432 | bytes 9437184 | tf_op jit(solution)/shard_map/add | solution.py:327
Async XLA Ops:
  0.0 118.6 %copy-start = (f32[8,3,128,2,128]{4,3,2,1,0:T(2,128)S(1)}, f32[8,3,128,2,128]{4,3,2,1,0:T(2,128)}, u32[]{:S(2)}) copy-start(f32[8,3,128,2,128]{4,3,2,1,0:T(2,128)} %param.5) | copy-start | bytes 9437188

commit v5 on v4

--- a/solution.py
+++ b/solution.py
@@ -322,7 +322,7 @@
             dma((NQ, 2)), dma((NQ, 2)),
             dma((NQ, 2)), dma((NQ, 2)),
         ],
-        compiler_params=pltpu.CompilerParams(collective_id=0, has_side_effects=True, vmem_limit_bytes=60 << 20),
+        compiler_params=pltpu.CompilerParams(collective_id=0, has_side_effects=True, vmem_limit_bytes=36 << 20),
     )(left, right)
     return (res + out).reshape(residual_in.shape)
 

time: 123 us -> 127 us (1.033)
  Pallas kernels: 119 us -> 122 us
  local copies, waits for them, and re-layouts: 0.01 us -> 3 us
  other arithmetic: 3.87 us -> 1.98 us
    pallas_call x1, Pallas kernels: 119 us -> 122 us  [per_device(): pl.pallas_call(kernel, out_shape=jax.ShapeDtypeStruct(res.shape, jnp.floa...]
    unnamed x2 -> x6, local copies, waits for them, and re-layouts: 0.01 us -> 3 us
    add x1, other arithmetic: 3.87 us -> 1.98 us  [per_device(): return (res + out).reshape(residual_in.shape)]
where the time goes in v5:
time: 127 us
  Pallas kernels  122 us (96%)
  local copies, waits for them, and re-layouts  3 us (2%)
  other arithmetic  1.98 us (2%)
    pallas_call x1, Pallas kernels, per_device(): pl.pallas_call(kernel, out_shape=jax.ShapeDtypeStruct(res.shape, jnp.floa...  122 us
    unnamed x6, local copies, waits for them, and re-layouts  3 us

profile of v5, /device:TPU:3, one launch (start us, length us, event | category | flops | bytes accessed | tf_op | source)
XLA Modules:
  0.0 127.3 jit_solution(1294869415146611317)
XLA Ops:
  0.0 0.0 copy-start
  0.0 1.6 %copy-done = bf16[1,2,128,32,128]{4,3,2,1,0:T(8,128)(2,1)S(1)} copy-done((bf16[1,2,128,32,128]{4,3,2,1,0:T(8,128)(2,1)S(1)}, bf16[1,2,128,32,128]{4,3,2,1,0:T(8,128)(2,1)}, u32[]{:S(2)}) %copy-start) | copy-done | bytes 2097176
  1.6 0.0 copy-start.1
  1.6 1.4 %copy-done.1 = bf16[8,3,128,2,128]{4,3,2,1,0:T(2,128)(2,1)S(1)} copy-done((bf16[8,3,128,2,128]{4,3,2,1,0:T(2,128)(2,1)S(1)}, bf16[8,3,128,2,128]{4,3,2,1,0:T(2,128)(2,1)}, u32[]{:S(2)}) %copy-start.1) | copy-done | bytes 1572888
  3.0 0.0 copy-start.2
  3.0 122.3 %shard_map.37 = f32[8,768,128]{2,1,0:T(8,128)S(1)} custom-call(bf16[8,768,128]{2,1,0:T(8,128)(2,1)S(1)} %bitcast.5, bf16[256,32,128]{2,1,0:T(8,128)(2,1)S(1)} %bitcast.4), custom_call_target="tpu_custom_call" | custom-call | tf_op jit(solution)/shard_map/pallas_call | solution.py:301
  125.3 0.0 copy-done.2
  125.3 2.0 %add.3 = f32[8,768,128]{2,1,0:T(8,128)} add(f32[8,768,128]{2,1,0:T(8,128)S(1)} %bitcast.6, f32[8,768,128]{2,1,0:T(8,128)S(1)} %shard_map.37) | non-fusion elementwise | flops 786432 | bytes 9437184 | tf_op jit(solution)/shard_map/add | solution.py:327
Async XLA Ops:
  0.0 1.6 %copy-start = (bf16[1,2,128,32,128]{4,3,2,1,0:T(8,128)(2,1)S(1)}, bf16[1,2,128,32,128]{4,3,2,1,0:T(8,128)(2,1)}, u32[]{:S(2)}) copy-start(bf16[1,2,128,32,128]{4,3,2,1,0:T(8,128)(2,1)} %param.3) | copy-start | bytes 6291460
  1.6 1.4 %copy-start.1 = (bf16[8,3,128,2,128]{4,3,2,1,0:T(2,128)(2,1)S(1)}, bf16[8,3,128,2,128]{4,3,2,1,0:T(2,128)(2,1)}, u32[]{:S(2)}) copy-start(bf16[8,3,128,2,128]{4,3,2,1,0:T(2,128)(2,1)} %param.4) | copy-start | bytes 4718596
  3.0 122.3 %copy-start.2 = (f32[8,3,128,2,128]{4,3,2,1,0:T(2,128)S(1)}, f32[8,3,128,2,128]{4,3,2,1,0:T(2,128)}, u32[]{:S(2)}) copy-start(f32[8,3,128,2,128]{4,3,2,1,0:T(2,128)} %param.5) | copy-start | bytes 9437188

commit v6 on v5

--- a/solution.py
+++ b/solution.py
@@ -323,7 +323,7 @@
             dma((NQ, 2)), dma((NQ, 2)),
         ],
         compiler_params=pltpu.CompilerParams(collective_id=0, has_side_effects=True, vmem_limit_bytes=36 << 20),
-    )(left, right)
+    )(pltpu.with_memory_space_constraint(left, pltpu.HBM), pltpu.with_memory_space_constraint(right, pltpu.HBM))
     return (res + out).reshape(residual_in.shape)
 
 

time: 127 us -> 121 us (0.953)
  Pallas kernels: 122 us -> 119 us
  local copies, waits for them, and re-layouts: 3 us -> 0.01 us
    pallas_call x1, Pallas kernels: 122 us -> 119 us  [per_device(): pl.pallas_call(kernel, out_shape=jax.ShapeDtypeStruct(res.shape, jnp.floa...]
    unnamed x6 -> x2, local copies, waits for them, and re-layouts: 3 us -> 0.01 us
where the time goes in v6:
time: 121 us
  Pallas kernels  119 us (98%)
  other arithmetic  1.98 us (2%)
    pallas_call x1, Pallas kernels, per_device(): pl.pallas_call(kernel, out_shape=jax.ShapeDtypeStruct(res.shape, jnp.floa...  119 us

profile of v6, /device:TPU:3, one launch (start us, length us, event | category | flops | bytes accessed | tf_op | source)
XLA Modules:
  0.0 120.8 jit_solution(14211185405540883655)
XLA Ops:
  0.0 0.0 copy-start
  0.0 118.8 %shard_map.37 = f32[8,768,128]{2,1,0:T(8,128)S(1)} custom-call(bf16[8,768,128]{2,1,0:T(8,128)(2,1)} %bitcast.6, bf16[256,32,128]{2,1,0:T(8,128)(2,1)} %bitcast.5), custom_call_target="tpu_custom_call" | custom-call | tf_op jit(solution)/shard_map/pallas_call | solution.py:301
  118.8 0.0 copy-done
  118.8 2.0 %add.3 = f32[8,768,128]{2,1,0:T(8,128)} add(f32[8,768,128]{2,1,0:T(8,128)S(1)} %bitcast.4, f32[8,768,128]{2,1,0:T(8,128)S(1)} %shard_map.37) | non-fusion elementwise | flops 786432 | bytes 9437184 | tf_op jit(solution)/shard_map/add | solution.py:327
Async XLA Ops:
  0.0 118.8 %copy-start = (f32[8,3,128,2,128]{4,3,2,1,0:T(2,128)S(1)}, f32[8,3,128,2,128]{4,3,2,1,0:T(2,128)}, u32[]{:S(2)}) copy-start(f32[8,3,128,2,128]{4,3,2,1,0:T(2,128)} %param.5) | copy-start | bytes 9437188

commit v7 on v6

--- a/solution.py
+++ b/solution.py
@@ -16,11 +16,12 @@
 LINES = 2 * sum(n for _, _, n in CHUNKS)
 PIECES = (4, 1, 1, 2)
 PLAN = (
-    "AS0", "BS1", "BL0", "BS0", "AS1", "GS0", "AS2", "BA1", "GF0", "AS3", "GS1", "BL2", "BL3", "GR0", "P01",
-    "BA0", "AS4", "GS2", "GF1", "P00", "AS5", "GS3", "BS3", "BS2", "GF2", "GR1", "P1", "AS6", "GS4", "GF3", "GR2",
-    "P2", "BA3", "BA2", "F01", "F00", "AS7", "GS5", "GF4", "GR3", "P3", "F11", "F10", "GS6", "GF5", "GR4", "P4",
-    "F21", "F20", "GS7", "GF6", "GR5", "P5", "F31", "F30", "GF7", "GR6", "P6", "F41", "F40", "GR7", "P7", "F51",
-    "F50", "O61", "O60", "O71", "O70", "Z", "W61", "W60", "W71", "W70",
+    "AS0", "BS1", "BL0", "BS0", "AS1", "AL2", "AL3", "AL4", "AL5", "AL6", "AL7", "BL3", "BL2", "GS0", "AS2",
+    "BA1", "GF0", "AS3", "GS1", "GR0", "P01", "BA0", "AS4", "GS2", "GF1", "P00", "AS5", "GS3", "BS3", "BS2",
+    "GF2", "GR1", "P1", "AS6", "GS4", "GF3", "GR2", "P2", "BA3", "BA2", "F01", "F00", "AS7", "GS5", "GF4", "GR3",
+    "P3", "F11", "F10", "GS6", "GF5", "GR4", "P4", "F21", "F20", "GS7", "GF6", "GR5", "P5", "F31", "F30", "GF7",
+    "GR6", "P6", "F41", "F40", "GR7", "P7", "F51", "F50", "O61", "O60", "O71", "O70", "Z", "W61", "W60", "W71",
+    "W70",
 )
 
 
@@ -172,7 +173,7 @@
     def a_start(q):
         dx, off, n = CHUNKS[q]
         hx = (x + 4 - dx) % 4
-        if q:
+        if q and "AL" + str(q) not in PLAN:
             a_lay(q)
         for zz in (1, 0):
             if dx or zz:
@@ -257,7 +258,7 @@
         cf[j, lines_of(q), :] += cr[j, lines_of(q), :]
         final_copy(q, j).start()
 
-    steps = dict(AS=a_start, BL=b_lay, BA=b_arrive, GS=gather_start, GF=gather_forward, GR=gather_rest)
+    steps = dict(AL=a_lay, AS=a_start, BL=b_lay, BA=b_arrive, GS=gather_start, GF=gather_forward, GR=gather_rest)
     for step in PLAN:
         args = [int(d) for d in step if d.isdigit()]
         name = step.rstrip("0123456789")

time: 121 us -> 121 us (level)
  no operation moved by 1% of the time
where the time goes in v7:
time: 121 us
  Pallas kernels  119 us (98%)
  other arithmetic  1.98 us (2%)
    pallas_call x1, Pallas kernels, per_device(): pl.pallas_call(kernel, out_shape=jax.ShapeDtypeStruct(res.shape, jnp.floa...  119 us

profile of v7, /device:TPU:3, one launch (start us, length us, event | category | flops | bytes accessed | tf_op | source)
XLA Modules:
  0.0 120.8 jit_solution(7692814905330608048)
XLA Ops:
  0.0 0.0 copy-start
  0.0 118.8 %shard_map.37 = f32[8,768,128]{2,1,0:T(8,128)S(1)} custom-call(bf16[8,768,128]{2,1,0:T(8,128)(2,1)} %bitcast.6, bf16[256,32,128]{2,1,0:T(8,128)(2,1)} %bitcast.5), custom_call_target="tpu_custom_call" | custom-call | tf_op jit(solution)/shard_map/pallas_call | solution.py:302
  118.8 0.0 copy-done
  118.8 2.0 %add.3 = f32[8,768,128]{2,1,0:T(8,128)} add(f32[8,768,128]{2,1,0:T(8,128)S(1)} %bitcast.4, f32[8,768,128]{2,1,0:T(8,128)S(1)} %shard_map.37) | non-fusion elementwise | flops 786432 | bytes 9437184 | tf_op jit(solution)/shard_map/add | solution.py:328
Async XLA Ops:
  0.0 118.8 %copy-start = (f32[8,3,128,2,128]{4,3,2,1,0:T(2,128)S(1)}, f32[8,3,128,2,128]{4,3,2,1,0:T(2,128)}, u32[]{:S(2)}) copy-start(f32[8,3,128,2,128]{4,3,2,1,0:T(2,128)} %param.5) | copy-start | bytes 9437188

commit v8 on v7

--- a/solution.py
+++ b/solution.py
@@ -17,8 +17,8 @@
 PIECES = (4, 1, 1, 2)
 PLAN = (
     "AS0", "BS1", "BL0", "BS0", "AS1", "AL2", "AL3", "AL4", "AL5", "AL6", "AL7", "BL3", "BL2", "GS0", "AS2",
-    "BA1", "GF0", "AS3", "GS1", "GR0", "P01", "BA0", "AS4", "GS2", "GF1", "P00", "AS5", "GS3", "BS3", "BS2",
-    "GF2", "GR1", "P1", "AS6", "GS4", "GF3", "GR2", "P2", "BA3", "BA2", "F01", "F00", "AS7", "GS5", "GF4", "GR3",
+    "BA1", "GF0", "AS3", "GS1", "GR0", "P01", "BA0", "AS4", "GS2", "GF1", "P00", "AS5", "GS3", "GF2", "BS3",
+    "BS2", "GR1", "P1", "AS6", "GS4", "GF3", "GR2", "P2", "BA3", "BA2", "F01", "F00", "AS7", "GS5", "GF4", "GR3",
     "P3", "F11", "F10", "GS6", "GF5", "GR4", "P4", "F21", "F20", "GS7", "GF6", "GR5", "P5", "F31", "F30", "GF7",
     "GR6", "P6", "F41", "F40", "GR7", "P7", "F51", "F50", "O61", "O60", "O71", "O70", "Z", "W61", "W60", "W71",
     "W70",

time: 121 us -> 122 us (level)
  no operation moved by 1% of the time
where the time goes in v8:
time: 122 us
  Pallas kernels  120 us (98%)
  other arithmetic  1.98 us (2%)
    pallas_call x1, Pallas kernels, per_device(): pl.pallas_call(kernel, out_shape=jax.ShapeDtypeStruct(res.shape, jnp.floa...  120 us

profile of v8, /device:TPU:3, one launch (start us, length us, event | category | flops | bytes accessed | tf_op | source)
XLA Modules:
  0.0 121.7 jit_solution(7413578472500992186)
XLA Ops:
  0.0 0.0 copy-start
  0.0 119.7 %shard_map.37 = f32[8,768,128]{2,1,0:T(8,128)S(1)} custom-call(bf16[8,768,128]{2,1,0:T(8,128)(2,1)} %bitcast.6, bf16[256,32,128]{2,1,0:T(8,128)(2,1)} %bitcast.5), custom_call_target="tpu_custom_call" | custom-call | tf_op jit(solution)/shard_map/pallas_call | solution.py:302
  119.8 0.0 copy-done
  119.8 2.0 %add.3 = f32[8,768,128]{2,1,0:T(8,128)} add(f32[8,768,128]{2,1,0:T(8,128)S(1)} %bitcast.4, f32[8,768,128]{2,1,0:T(8,128)S(1)} %shard_map.37) | non-fusion elementwise | flops 786432 | bytes 9437184 | tf_op jit(solution)/shard_map/add | solution.py:328
Async XLA Ops:
  0.0 119.8 %copy-start = (f32[8,3,128,2,128]{4,3,2,1,0:T(2,128)S(1)}, f32[8,3,128,2,128]{4,3,2,1,0:T(2,128)}, u32[]{:S(2)}) copy-start(f32[8,3,128,2,128]{4,3,2,1,0:T(2,128)} %param.5) | copy-start | bytes 9437188
